TPU v7x, 32 devices: a whole 2x2x4 slice. The times are simulated.
32 devices in a mesh: row: 4 (over y, x), col: 8 (over z, core).
Axes of the slice: x: 2, y: 2, z: 4, core: 2. Of those that a mesh axis runs over, the one named last changes fastest.
Arguments:
- train_inputs: bfloat16 [512, 8192], P(('row', 'col')), may hold values from -6 to 6
- train_grads: bfloat16 [512, 8192], P(('row', 'col')), may hold values from -6 to 6
- query_inputs: bfloat16 [256, 8192], P(('row', 'col')), may hold values from -6 to 6
- query_grads: bfloat16 [256, 8192], P(('row', 'col')), may hold values from -6 to 6
- input_basis: bfloat16 [8192, 8192], P('row', 'col'), may hold values from -0.0625 to 0.0625
- output_basis: bfloat16 [8192, 8192], P('col', 'row'), may hold values from -0.0625 to 0.0625
- eigenvalues: float32 [8192, 8192], P('row', 'col'), may hold values from 0.5 to 5
- query_starts: int32 [16], replicated, may hold values from 0 to 255, as said below
- query_ends: int32 [16], replicated, may hold values from 1 to 256, as said below
Outputs:
- scores: float32 [16, 512], replicated
Inputs may be any that keep to these rules, and one draw needn't show every extreme that they name: Query q covers the query rows query_starts[q] <= r < query_ends[q]: a nonempty span of at most 128 rows that lies inside one aligned block of 128 rows (rows k * 128 to (k + 1) * 128 - 1); spans of different queries may intersect or share a block. `query_ends`: see query_starts.
All inputs are finite; a program needn't handle non-finite values.
Results may differ from a plain program's by a relative error of at most 0.005.
Values may be sent and summed in bfloat16 or wider, within the bound.
No kernel may reach another device: no remote copies, remote signals or barrier semaphores. Data moves between devices by JAX's collectives and lax.ppermute only.
A program may use at most 64 MiB of HBM per device.

v0:
```python
import math

import jax
import jax.numpy as jnp
from jax import lax
from jax.sharding import PartitionSpec as P

D_IN = 8192
D_OUT = 8192
QBLOCK = 128


damping = 0.1


def shards(
    train_inputs,
    train_grads,
    query_inputs,
    query_grads,
    input_basis,
    output_basis,
    eigenvalues,
    query_starts,
    query_ends,
):
    grouped = (
        lax.all_gather(train_inputs, "col", axis=0, tiled=True),
        lax.all_gather(query_inputs, "col", axis=0, tiled=True),
    )
    train_in, query_in = (
        lax.all_to_all(grouped[0], "row", split_axis=1, concat_axis=0, tiled=True),
        lax.all_to_all(grouped[1], "row", split_axis=1, concat_axis=0, tiled=True),
    )
    spread = (
        lax.all_to_all(train_grads, "col", split_axis=1, concat_axis=0, tiled=True),
        lax.all_to_all(query_grads, "col", split_axis=1, concat_axis=0, tiled=True),
    )
    train_out, query_out = (
        lax.all_gather(spread[0], "row", axis=0, tiled=True),
        lax.all_gather(spread[1], "row", axis=0, tiled=True),
    )
    train_in_part = jnp.dot(train_in, input_basis, preferred_element_type=jnp.float32)
    query_in_part = jnp.dot(query_in, input_basis, preferred_element_type=jnp.float32)
    train_out_part = jnp.dot(train_out, output_basis, preferred_element_type=jnp.float32)
    query_out_part = jnp.dot(query_out, output_basis, preferred_element_type=jnp.float32)
    in_sums = lax.psum((train_in_part, query_in_part), "row")
    out_sums = lax.psum((train_out_part, query_out_part), "col")
    train_in_rot = in_sums[0].astype(jnp.bfloat16)
    query_in_rot = in_sums[1].astype(jnp.bfloat16)
    train_grad_rot = out_sums[0].astype(jnp.bfloat16)
    query_grad_rot = out_sums[1].astype(jnp.bfloat16)
    grads_wide = train_grad_rot.astype(jnp.float32)
    denominator = eigenvalues + damping

    def per_query(span):
        span_start, span_end = span
        block_top = span_start // QBLOCK * QBLOCK
        grad_rows = lax.dynamic_slice_in_dim(query_grad_rot, block_top, QBLOCK, 0)
        input_rows = lax.dynamic_slice_in_dim(query_in_rot, block_top, QBLOCK, 0)
        positions = block_top + jnp.arange(QBLOCK, dtype=jnp.int32)
        inside = (positions >= span_start) & (positions < span_end)
        grad_rows = jnp.where(inside[:, None], grad_rows, jnp.zeros((), grad_rows.dtype))
        outer_sum = lax.dot_general(
            grad_rows, input_rows, (((0,), (0,)), ((), ())), preferred_element_type=jnp.float32
        )
        scaled = (outer_sum / denominator).astype(jnp.bfloat16)
        paired = lax.dot_general(
            train_in_rot, scaled, (((1,), (1,)), ((), ())), preferred_element_type=jnp.float32
        )
        return jnp.sum(grads_wide * paired, axis=1)

    partial_scores = lax.map(per_query, (query_starts, query_ends))
    totals = lax.psum(partial_scores, ("row", "col"))
    return totals * (1.0 / math.sqrt(D_IN * D_OUT * QBLOCK))


def solution(mesh):
    in_specs = (
        P(("row", "col"), None),
        P(("row", "col"), None),
        P(("row", "col"), None),
        P(("row", "col"), None),
        P("row", "col"),
        P("col", "row"),
        P("row", "col"),
        P(),
        P(),
    )
    out_specs = P()
    return jax.shard_map(shards, mesh=mesh, in_specs=in_specs, out_specs=out_specs, check_vma=False)
```

profile of v0, /device:TPU:0, one launch (start us, length us, event | category | flops | bytes accessed | tf_op | source)
XLA Modules:
  0.0 640.9 jit_solution(6413890611103058480)
XLA Ops:
  8.3 18.5 %all_to_all.76 = bf16[16,8,1024]{2,0,1:T(8,128)(2,1)} all-to-all(bf16[16,8,1024]{2,0,1:T(8,128)(2,1)S(1)} %bitcast.52), channel_id=1, replica_groups=mesh['row'=4,'col'=8] {'col'}, dimensions={1} | all-to-all | bytes 524288 | tf_op jit(solution)/shard_map/all_to_all | solution.py:36
  31.0 8.6 %broadcast_add_fusion = f32[2048,1024]{1,0:T(8,128)} fusion(f32[2048,1024]{1,0:T(8,128)} %param.17), kind=kLoop, calls=%fused_computation.13 | loop fusion | flops 2097152 | bytes 16777216 | tf_op jit(solution)/shard_map/add | solution.py:54
  39.6 13.4 %all_gather.12 = bf16[256,1024]{1,0:T(8,128)(2,1)S(1)} all-gather(bf16[64,1024]{1,0:T(8,128)(2,1)S(1)} %bitcast.53), channel_id=1, replica_groups=mesh['row'=4,'col'=8] {'row'}, dimensions={0}, use_global_device_ids=true | all-gather | bytes 655360 | tf_op jit(solution)/shard_map/all_gather | solution.py:41
  58.9 4.7 fusion.18
  63.6 12.0 %all-gather.8.cloned.1.call-done = bf16[512,1024]{1,0:T(8,128)(2,1)} async-done(((bf16[128,1024]{1,0:T(8,128)(2,1)}), bf16[512,1024]{1,0:T(8,128)(2,1)}) %all-gather.8.cloned.1.call-update) | async-done | bytes 1048592 | tf_op jit(solution)/shard_map/all_gather | solution.py:40
  75.6 6.8 %fusion.21 = f32[512,2048]{1,0:T(8,128)} fusion(bf16[512,1024]{1,0:T(8,128)(2,1)} %all-gather.8.cloned.1.call-done, bf16[1024,2048]{1,0:T(8,128)(2,1)} %param.16), kind=kOutput, calls=%fused_computation.21 | convolution fusion | flops 2147483648 | bytes 9437184 | tf_op jit(solution)/shard_map/dot_general | solution.py:45
  82.5 24.0 %all-gather.6.cloned.1.call-done = bf16[128,8192]{1,0:T(8,128)(2,1)} async-done(((bf16[16,8192]{1,0:T(8,128)(2,1)}), bf16[128,8192]{1,0:T(8,128)(2,1)}) %all-gather.6.cloned.1.call-update) | async-done | bytes 2097168 | tf_op jit(solution)/shard_map/all_gather | solution.py:28
  106.4 4.0 copy.18
  110.5 3.6 all-to-all-start.2
  114.1 128.7 %all-reduce.4 = (bf16[256,2048]{1,0:T(8,128)(2,1)}, bf16[512,2048]{1,0:T(8,128)(2,1)}) all-reduce(f32[256,2048]{1,0:T(8,128)} %fusion.18, f32[512,2048]{1,0:T(8,128)} %fusion.21), channel_id=1, replica_groups=mesh['row'=4,'col'=8] {'col'}, use_global_device_ids=true, to_apply=%region_0.0 | all-reduce | flops 1572864 | bytes 9437184 | tf_op jit(solution)/shard_map/psum | solution.py:48
  242.9 4.2 copy.21
  247.0 3.8 fusion.19
  253.5 5.2 fusion.20
  258.7 111.6 %all-reduce.5 = (bf16[256,1024]{1,0:T(8,128)(2,1)}, bf16[512,1024]{1,0:T(8,128)(2,1)}) all-reduce(f32[256,1024]{1,0:T(8,128)S(1)} %fusion.19, f32[512,1024]{1,0:T(8,128)S(1)} %fusion.20), channel_id=1, replica_groups=mesh['row'=4,'col'=8] {'row'}, use_global_device_ids=true, to_apply=%region_1.0 | all-reduce | flops 786432 | bytes 4718592 | tf_op jit(solution)/shard_map/psum | solution.py:47
  370.3 225.3 %while.12 = (s32[]{:T(128)}, f32[16,512]{1,0:T(8,128)S(1)}, s32[16]{0:T(128)S(1)}, s32[16]{0:T(128)S(1)}, bf16[256,2048]{1,0:T(8,128)(2,1)}, /*index=5*/bf16[256...) while((s32[]{:T(128)}, f32[16,512]{1,0:T(8,128)S(1)}, ...), condition=%wide.region_6.7_spmd, body=%wide.region_4.6_spmd.sunk | while | flops 2690908160 | bytes 14425729 | solution.py:73
  375.5 8.8 %fusion.38 = f32[512]{0:T(512)S(1)} fusion(f32[512,2048]{0,1:T(8,128)} %get-tuple-element.273, bf16[512,1024]{1,0:T(8,128)(2,1)} %get-tuple-element.272, f32[2048,1024]{1,0:T(8,128)} %get-tuple-element.271, bf16[256,2048]{1,0:T(8,128)(2,1)} %get-tuple-element.269, s32[]{:T(128)S(6)} %select_n.30, pred[128]{0:T(512)(128)(4,1)S(1)} %compare_and_fusion.2, ...), kind=kOutput, calls=%fused_computation.2.clone.1 | convolution fusion | flops 2690907648 | bytes 14421120 | tf_op jit(solution)/shard_map/while/body/eval_jaxpr/dot_general | solution.py:68
  389.6 8.8 %fusion.38 = f32[512]{0:T(512)S(1)} fusion(f32[512,2048]{0,1:T(8,128)} %get-tuple-element.273, bf16[512,1024]{1,0:T(8,128)(2,1)} %get-tuple-element.272, f32[2048,1024]{1,0:T(8,128)} %get-tuple-element.271, bf16[256,2048]{1,0:T(8,128)(2,1)} %get-tuple-element.269, s32[]{:T(128)S(6)} %select_n.30, pred[128]{0:T(512)(128)(4,1)S(1)} %compare_and_fusion.2, ...), kind=kOutput, calls=%fused_computation.2.clone.1 | convolution fusion | flops 2690907648 | bytes 14421120 | tf_op jit(solution)/shard_map/while/body/eval_jaxpr/dot_general | solution.py:68
  403.7 8.8 %fusion.38 = f32[512]{0:T(512)S(1)} fusion(f32[512,2048]{0,1:T(8,128)} %get-tuple-element.273, bf16[512,1024]{1,0:T(8,128)(2,1)} %get-tuple-element.272, f32[2048,1024]{1,0:T(8,128)} %get-tuple-element.271, bf16[256,2048]{1,0:T(8,128)(2,1)} %get-tuple-element.269, s32[]{:T(128)S(6)} %select_n.30, pred[128]{0:T(512)(128)(4,1)S(1)} %compare_and_fusion.2, ...), kind=kOutput, calls=%fused_computation.2.clone.1 | convolution fusion | flops 2690907648 | bytes 14421120 | tf_op jit(solution)/shard_map/while/body/eval_jaxpr/dot_general | solution.py:68
  417.7 8.8 %fusion.38 = f32[512]{0:T(512)S(1)} fusion(f32[512,2048]{0,1:T(8,128)} %get-tuple-element.273, bf16[512,1024]{1,0:T(8,128)(2,1)} %get-tuple-element.272, f32[2048,1024]{1,0:T(8,128)} %get-tuple-element.271, bf16[256,2048]{1,0:T(8,128)(2,1)} %get-tuple-element.269, s32[]{:T(128)S(6)} %select_n.30, pred[128]{0:T(512)(128)(4,1)S(1)} %compare_and_fusion.2, ...), kind=kOutput, calls=%fused_computation.2.clone.1 | convolution fusion | flops 2690907648 | bytes 14421120 | tf_op jit(solution)/shard_map/while/body/eval_jaxpr/dot_general | solution.py:68
  431.8 8.8 %fusion.38 = f32[512]{0:T(512)S(1)} fusion(f32[512,2048]{0,1:T(8,128)} %get-tuple-element.273, bf16[512,1024]{1,0:T(8,128)(2,1)} %get-tuple-element.272, f32[2048,1024]{1,0:T(8,128)} %get-tuple-element.271, bf16[256,2048]{1,0:T(8,128)(2,1)} %get-tuple-element.269, s32[]{:T(128)S(6)} %select_n.30, pred[128]{0:T(512)(128)(4,1)S(1)} %compare_and_fusion.2, ...), kind=kOutput, calls=%fused_computation.2.clone.1 | convolution fusion | flops 2690907648 | bytes 14421120 | tf_op jit(solution)/shard_map/while/body/eval_jaxpr/dot_general | solution.py:68
  445.9 8.8 %fusion.38 = f32[512]{0:T(512)S(1)} fusion(f32[512,2048]{0,1:T(8,128)} %get-tuple-element.273, bf16[512,1024]{1,0:T(8,128)(2,1)} %get-tuple-element.272, f32[2048,1024]{1,0:T(8,128)} %get-tuple-element.271, bf16[256,2048]{1,0:T(8,128)(2,1)} %get-tuple-element.269, s32[]{:T(128)S(6)} %select_n.30, pred[128]{0:T(512)(128)(4,1)S(1)} %compare_and_fusion.2, ...), kind=kOutput, calls=%fused_computation.2.clone.1 | convolution fusion | flops 2690907648 | bytes 14421120 | tf_op jit(solution)/shard_map/while/body/eval_jaxpr/dot_general | solution.py:68
  460.0 8.8 %fusion.38 = f32[512]{0:T(512)S(1)} fusion(f32[512,2048]{0,1:T(8,128)} %get-tuple-element.273, bf16[512,1024]{1,0:T(8,128)(2,1)} %get-tuple-element.272, f32[2048,1024]{1,0:T(8,128)} %get-tuple-element.271, bf16[256,2048]{1,0:T(8,128)(2,1)} %get-tuple-element.269, s32[]{:T(128)S(6)} %select_n.30, pred[128]{0:T(512)(128)(4,1)S(1)} %compare_and_fusion.2, ...), kind=kOutput, calls=%fused_computation.2.clone.1 | convolution fusion | flops 2690907648 | bytes 14421120 | tf_op jit(solution)/shard_map/while/body/eval_jaxpr/dot_general | solution.py:68
  474.1 8.8 %fusion.38 = f32[512]{0:T(512)S(1)} fusion(f32[512,2048]{0,1:T(8,128)} %get-tuple-element.273, bf16[512,1024]{1,0:T(8,128)(2,1)} %get-tuple-element.272, f32[2048,1024]{1,0:T(8,128)} %get-tuple-element.271, bf16[256,2048]{1,0:T(8,128)(2,1)} %get-tuple-element.269, s32[]{:T(128)S(6)} %select_n.30, pred[128]{0:T(512)(128)(4,1)S(1)} %compare_and_fusion.2, ...), kind=kOutput, calls=%fused_computation.2.clone.1 | convolution fusion | flops 2690907648 | bytes 14421120 | tf_op jit(solution)/shard_map/while/body/eval_jaxpr/dot_general | solution.py:68
  488.1 8.8 %fusion.38 = f32[512]{0:T(512)S(1)} fusion(f32[512,2048]{0,1:T(8,128)} %get-tuple-element.273, bf16[512,1024]{1,0:T(8,128)(2,1)} %get-tuple-element.272, f32[2048,1024]{1,0:T(8,128)} %get-tuple-element.271, bf16[256,2048]{1,0:T(8,128)(2,1)} %get-tuple-element.269, s32[]{:T(128)S(6)} %select_n.30, pred[128]{0:T(512)(128)(4,1)S(1)} %compare_and_fusion.2, ...), kind=kOutput, calls=%fused_computation.2.clone.1 | convolution fusion | flops 2690907648 | bytes 14421120 | tf_op jit(solution)/shard_map/while/body/eval_jaxpr/dot_general | solution.py:68
  502.2 8.8 %fusion.38 = f32[512]{0:T(512)S(1)} fusion(f32[512,2048]{0,1:T(8,128)} %get-tuple-element.273, bf16[512,1024]{1,0:T(8,128)(2,1)} %get-tuple-element.272, f32[2048,1024]{1,0:T(8,128)} %get-tuple-element.271, bf16[256,2048]{1,0:T(8,128)(2,1)} %get-tuple-element.269, s32[]{:T(128)S(6)} %select_n.30, pred[128]{0:T(512)(128)(4,1)S(1)} %compare_and_fusion.2, ...), kind=kOutput, calls=%fused_computation.2.clone.1 | convolution fusion | flops 2690907648 | bytes 14421120 | tf_op jit(solution)/shard_map/while/body/eval_jaxpr/dot_general | solution.py:68
  516.3 8.8 %fusion.38 = f32[512]{0:T(512)S(1)} fusion(f32[512,2048]{0,1:T(8,128)} %get-tuple-element.273, bf16[512,1024]{1,0:T(8,128)(2,1)} %get-tuple-element.272, f32[2048,1024]{1,0:T(8,128)} %get-tuple-element.271, bf16[256,2048]{1,0:T(8,128)(2,1)} %get-tuple-element.269, s32[]{:T(128)S(6)} %select_n.30, pred[128]{0:T(512)(128)(4,1)S(1)} %compare_and_fusion.2, ...), kind=kOutput, calls=%fused_computation.2.clone.1 | convolution fusion | flops 2690907648 | bytes 14421120 | tf_op jit(solution)/shard_map/while/body/eval_jaxpr/dot_general | solution.py:68
  530.4 8.8 %fusion.38 = f32[512]{0:T(512)S(1)} fusion(f32[512,2048]{0,1:T(8,128)} %get-tuple-element.273, bf16[512,1024]{1,0:T(8,128)(2,1)} %get-tuple-element.272, f32[2048,1024]{1,0:T(8,128)} %get-tuple-element.271, bf16[256,2048]{1,0:T(8,128)(2,1)} %get-tuple-element.269, s32[]{:T(128)S(6)} %select_n.30, pred[128]{0:T(512)(128)(4,1)S(1)} %compare_and_fusion.2, ...), kind=kOutput, calls=%fused_computation.2.clone.1 | convolution fusion | flops 2690907648 | bytes 14421120 | tf_op jit(solution)/shard_map/while/body/eval_jaxpr/dot_general | solution.py:68
  544.5 8.8 %fusion.38 = f32[512]{0:T(512)S(1)} fusion(f32[512,2048]{0,1:T(8,128)} %get-tuple-element.273, bf16[512,1024]{1,0:T(8,128)(2,1)} %get-tuple-element.272, f32[2048,1024]{1,0:T(8,128)} %get-tuple-element.271, bf16[256,2048]{1,0:T(8,128)(2,1)} %get-tuple-element.269, s32[]{:T(128)S(6)} %select_n.30, pred[128]{0:T(512)(128)(4,1)S(1)} %compare_and_fusion.2, ...), kind=kOutput, calls=%fused_computation.2.clone.1 | convolution fusion | flops 2690907648 | bytes 14421120 | tf_op jit(solution)/shard_map/while/body/eval_jaxpr/dot_general | solution.py:68
  558.5 8.8 %fusion.38 = f32[512]{0:T(512)S(1)} fusion(f32[512,2048]{0,1:T(8,128)} %get-tuple-element.273, bf16[512,1024]{1,0:T(8,128)(2,1)} %get-tuple-element.272, f32[2048,1024]{1,0:T(8,128)} %get-tuple-element.271, bf16[256,2048]{1,0:T(8,128)(2,1)} %get-tuple-element.269, s32[]{:T(128)S(6)} %select_n.30, pred[128]{0:T(512)(128)(4,1)S(1)} %compare_and_fusion.2, ...), kind=kOutput, calls=%fused_computation.2.clone.1 | convolution fusion | flops 2690907648 | bytes 14421120 | tf_op jit(solution)/shard_map/while/body/eval_jaxpr/dot_general | solution.py:68
  572.6 8.8 %fusion.38 = f32[512]{0:T(512)S(1)} fusion(f32[512,2048]{0,1:T(8,128)} %get-tuple-element.273, bf16[512,1024]{1,0:T(8,128)(2,1)} %get-tuple-element.272, f32[2048,1024]{1,0:T(8,128)} %get-tuple-element.271, bf16[256,2048]{1,0:T(8,128)(2,1)} %get-tuple-element.269, s32[]{:T(128)S(6)} %select_n.30, pred[128]{0:T(512)(128)(4,1)S(1)} %compare_and_fusion.2, ...), kind=kOutput, calls=%fused_computation.2.clone.1 | convolution fusion | flops 2690907648 | bytes 14421120 | tf_op jit(solution)/shard_map/while/body/eval_jaxpr/dot_general | solution.py:68
  586.7 8.8 %fusion.38 = f32[512]{0:T(512)S(1)} fusion(f32[512,2048]{0,1:T(8,128)} %get-tuple-element.273, bf16[512,1024]{1,0:T(8,128)(2,1)} %get-tuple-element.272, f32[2048,1024]{1,0:T(8,128)} %get-tuple-element.271, bf16[256,2048]{1,0:T(8,128)(2,1)} %get-tuple-element.269, s32[]{:T(128)S(6)} %select_n.30, pred[128]{0:T(512)(128)(4,1)S(1)} %compare_and_fusion.2, ...), kind=kOutput, calls=%fused_computation.2.clone.1 | convolution fusion | flops 2690907648 | bytes 14421120 | tf_op jit(solution)/shard_map/while/body/eval_jaxpr/dot_general | solution.py:68
  595.5 38.2 %psum.39 = f32[16,512]{1,0:T(8,128)S(1)} all-reduce(f32[16,512]{1,0:T(8,128)S(1)} %get-tuple-element.119), channel_id=1, replica_groups=mesh['row'=4,'col'=8] {'row','col'}, use_global_device_ids=true, to_apply=%region_7.8 | all-reduce | flops 8192 | bytes 65536 | tf_op jit(solution)/shard_map/psum | solution.py:74
  (87 shorter events, 58.5 us)
Async XLA Ops:
  6.5 46.5 %all-gather.4.cloned.1.call-start = ((), (), s32[]{:S(2)}) async-start(), calls=%async_computation.4 | async-start | bytes 1179648 | tf_op jit(solution)/shard_map/all_gather | solution.py:29
  7.3 68.4 %all-gather.8.cloned.1.call-start = ((), (), s32[]{:S(2)}) async-start(), calls=%async_computation.6 | async-start | bytes 1310720 | tf_op jit(solution)/shard_map/all_gather | solution.py:40
  26.8 79.6 %all-gather.6.cloned.1.call-start = ((), (), s32[]{:S(2)}) async-start(), calls=%async_computation.5 | async-start | bytes 2359296 | tf_op jit(solution)/shard_map/all_gather | solution.py:28
  27.6 12.0 %all-to-all-start = ((bf16[8,8,1024]{2,0,1:T(8,128)(2,1)}), bf16[8,8,1024]{2,0,1:T(8,128)(2,1)S(1)}, u32[]{:S(2)}, u32[]{:S(2)}) async-start(bf16[8,8,1024]{2,0,1:T(8,128)(2,1)} %bitcast.55), calls=%async_computation | async-start | bytes 262144 | tf_op jit(solution)/shard_map/all_to_all | solution.py:37
  55.3 55.2 %all-to-all-start.1 = ((bf16[64,4,2048]{2,0,1:T(8,128)(2,1)}), bf16[64,4,2048]{2,0,1:T(8,128)(2,1)S(1)}, u32[]{:S(2)}, u32[]{:S(2)}) async-start(bf16[64,4,2048]{2,0,1:T(8,128)(2,1)} %bitcast.35), calls=%async_computation.1 | async-start | bytes 2097152 | tf_op jit(solution)/shard_map/all_to_all | solution.py:33
  110.5 132.4 %copy-start = (bf16[64,4,2048]{2,0,1:T(8,128)(2,1)}, bf16[64,4,2048]{2,0,1:T(8,128)(2,1)S(1)}, u32[]{:S(2)}) copy-start(bf16[64,4,2048]{2,0,1:T(8,128)(2,1)S(1)} %all-to-all-done.1) | copy-start | bytes 3145732
  110.5 140.3 %all-to-all-start.2 = ((bf16[128,4,2048]{0,2,1:T(8,128)(2,1)}), bf16[128,4,2048]{0,2,1:T(8,128)(2,1)S(1)}, u32[]{:S(2)}, u32[]{:S(2)}) async-start(bf16[128,4,2048]{0,2,1:T(8,128)(2,1)} %bitcast.9), calls=%async_computation.2 | async-start | bytes 4194304 | tf_op jit(solution)/shard_map/all_to_all | solution.py:32
  253.5 116.8 %copy-start.1 = (s32[16]{0:T(128)S(1)}, s32[16]{0:T(128)}, u32[]{:S(2)}) copy-start(s32[16]{0:T(128)} %param.18) | copy-start | bytes 196
  253.5 116.8 %copy-start.2 = (s32[16]{0:T(128)S(1)}, s32[16]{0:T(128)}, u32[]{:S(2)}) copy-start(s32[16]{0:T(128)} %param.19) | copy-start | bytes 196
Sparse Core Ops, SparseCore 0:
  8.9 26.5 all-gather.3
  37.4 38.2 all-gather.7
  77.2 29.1 all-gather.5
where the time goes:
time: 643 us; the launch traced here: 641 us
  blocking collectives  310 us (48%)
  matrix products  161 us (25%)
  loops' own time  41.6 us (6%)
  waiting for transfers between devices  37.4 us (6%)
  local copies, waits for them, and re-layouts  36.4 us (6%)
  other arithmetic  30.5 us (5%)
  between operations  13.2 us (2%)
  starting transfers between devices  10.7 us (2%)
    dot_general x16, matrix products, per_query(): lax.dot_general(train_in_rot, scaled, (((1,), (1,)), ((), ())), preferred...  140 us
    psum x1, blocking collectives, shards(): out_sums = lax.psum((train_out_part, query_out_part), 'col')  129 us
    psum x1, blocking collectives, shards(): in_sums = lax.psum((train_in_part, query_in_part), 'row')  112 us
    another operation x1, loops' own time, shards(): partial_scores = lax.map(per_query, (query_starts, query_ends))  41.6 us
    psum x1, blocking collectives, shards(): totals = lax.psum(partial_scores, ('row', 'col'))  38.2 us
    all_gather x1, waiting for transfers between devices, shards(): lax.all_gather(train_inputs, 'col', axis=0, tiled=True)  24 us
    dynamic_slice x32, local copies, waits for them, and re-layouts, shards(): partial_scores = lax.map(per_query, (query_starts, query_ends))  21.2 us
    and x16, other arithmetic, per_query(): inside = (positions >= span_start) & (positions < span_end)  21.2 us
  transfers between devices with their start and end apart: 6, of which 2 were waited for; matrix products, arithmetic and copies ran while one was open for 6% of the time, Pallas kernels for 0%

commit v1 on v0

v1 whole, which is shorter than its diff:
```python
import functools
import math

import jax
import jax.numpy as jnp
from jax import lax
from jax.experimental import pallas as pl
from jax.experimental.pallas import tpu as pltpu
from jax.sharding import PartitionSpec as P


QBLOCK = 128
CHUNKS = (1, 1)
GROUPS = 2
damping = 0.1
bf16, f32 = jnp.bfloat16, jnp.float32


def swap(x, axis, k):
    if k == 0:
        return x
    return lax.ppermute(x, axis, [(i, i ^ k) for i in range(lax.axis_size(axis))])


def tree_sum(parts):
    while len(parts) > 1:
        parts = [parts[i] + parts[i + 1] for i in range(0, len(parts), 2)]
    return parts[0]


def global_rows(index, own, R, C, a, b):
    device, row = index // own, index % own
    return ((((device % R) ^ a) * C) + ((device // R) ^ b)) * own + row


def score_kernel(spans, ti_ref, qi_ref, *refs, n_queries, sizes, first, last):
    R, C, nt, nq = sizes
    if not first:
        init_ref, *refs = refs
    eig_ref, *refs = refs
    pieces, (out_ref, tiT_ref, d_ref, acc_ref) = refs[:C], refs[C:]
    step = pl.program_id(0)
    a, b = spans[2 * n_queries], spans[2 * n_queries + 1]

    @pl.when(step == 0)
    def _():
        acc_ref[...] = jnp.zeros_like(acc_ref)
        tiT_ref[...] = ti_ref[...].T

    d_ref[...] = 1.0 / (eig_ref[...] + damping)
    tg = jnp.concatenate([p[:R * nt, :] for p in pieces], axis=0).T.astype(f32)
    qg = jnp.concatenate([p[R * nt:, :] for p in pieces], axis=0).T
    pos = global_rows(lax.broadcasted_iota(jnp.int32, (1, R * C * nq), 1), nq, R, C, a, b)
    for q in range(n_queries):
        inside = (pos >= spans[q]) & (pos < spans[n_queries + q])
        mask = jnp.where(inside, 1.0, 0.0).astype(bf16)
        outer = jnp.dot(qg * mask, qi_ref[...], preferred_element_type=f32)
        scaled = (outer * d_ref[...]).astype(bf16)
        paired = jnp.dot(scaled, tiT_ref[...], preferred_element_type=f32)
        v = paired * tg
        acc_ref[q] += v.reshape(v.shape[0] // 8, 8, v.shape[1]).sum(0)

    @pl.when(step == pl.num_programs(0) - 1)
    def _():
        total = acc_ref[...].sum(1)
        if not first:
            total = total + init_ref[...]
        if last:
            n = total.shape[1]
            rows = global_rows(lax.broadcasted_iota(jnp.int32, (n, n), 0), nt, R, C, a, b)
            cols = lax.broadcasted_iota(jnp.int32, (n, n), 1)
            onehot = jnp.where(rows == cols, 1.0, 0.0).astype(f32)
            total = jnp.dot(total, onehot, preferred_element_type=f32, precision=lax.Precision.HIGHEST)
        out_ref[...] = total


def score(spans, ti, qi, init, eig, pieces, start, n_queries, sizes, last, block=256):
    T, I = ti.shape
    rows, width = pieces[0].shape
    block = min(block, width)
    whole = lambda arr: pl.BlockSpec(arr.shape, lambda i, *_: (0, 0))
    init = [] if init is None else [init]
    return pl.pallas_call(
        functools.partial(score_kernel, n_queries=n_queries, sizes=sizes, first=not init, last=last),
        out_shape=jax.ShapeDtypeStruct((n_queries, T), f32),
        grid_spec=pltpu.PrefetchScalarGridSpec(
            num_scalar_prefetch=1,
            grid=(width // block,),
            in_specs=[
                whole(ti), whole(qi), *map(whole, init),
                pl.BlockSpec((block, I), lambda i, *_: (start // block + i, 0)),
                *[pl.BlockSpec((rows, block), lambda i, *_: (0, i)) for _ in pieces],
            ],
            out_specs=pl.BlockSpec((n_queries, T), lambda i, *_: (0, 0)),
            scratch_shapes=[
                pltpu.VMEM((I, T), bf16),
                pltpu.VMEM((block, I), f32),
                pltpu.VMEM((n_queries, 8, T), f32),
            ],
        ),
        compiler_params=pltpu.CompilerParams(
            dimension_semantics=("arbitrary",), vmem_limit_bytes=56 << 20),
    )(spans, ti, qi, *init, eig, *pieces)


def shards(
    train_inputs,
    train_grads,
    query_inputs,
    query_grads,
    input_basis,
    output_basis,
    eigenvalues,
    query_starts,
    query_ends,
):
    R, C = lax.axis_size("row"), lax.axis_size("col")
    Z = C // 2
    a, b = lax.axis_index("row"), lax.axis_index("col")
    nt, nq = train_inputs.shape[0], query_inputs.shape[0]
    n = nt + nq
    K_in, I = input_basis.shape
    K_out, O = output_basis.shape
    n_queries = query_starts.shape[0]

    spans = jnp.concatenate([query_starts, query_ends, jnp.stack([a, b]).astype(jnp.int32)])

    x_in = jnp.concatenate([train_inputs, query_inputs], axis=0)
    in_a = [swap(lax.dynamic_slice_in_dim(x_in, (a ^ k) * K_in, K_in, 1), "row", k) for k in range(R)]
    x_out = jnp.concatenate([train_grads, query_grads], axis=0)
    parts = [lax.dynamic_slice_in_dim(x_out, (b ^ k) * K_out, K_out, 1) for k in range(C)]
    other = swap(jnp.concatenate(parts[1::2], axis=0), "col", 1)
    out_a = [swap(jnp.concatenate([parts[2 * z], other[z * n:(z + 1) * n]], axis=0), "col", 2 * z) for z in range(Z)]

    in_a = jnp.concatenate(in_a, axis=0)
    in_z = [swap(in_a, "col", 2 * z) for z in range(Z)]
    in_c = [swap(p, "col", 1) for p in in_z]
    out_a = jnp.concatenate(out_a, axis=0)
    out_r = [swap(out_a, "row", k) for k in range(R)]

    zs = Z // GROUPS

    def send_inputs(g):
        pieces = [p for z in range(g * zs, (g + 1) * zs) for p in (in_z[z], in_c[z])]
        rows = jnp.stack([p.reshape(R, n, K_in) for p in pieces], axis=1).reshape(R, 2 * zs * n, K_in)
        parts = []
        for k in range(R):
            parts.append(jnp.dot(rows[k], input_basis, preferred_element_type=f32))
        return [parts[0]] + [swap(parts[k], "row", k) for k in range(1, R)]

    def share_inputs(got):
        total = tree_sum(got).astype(bf16)
        return [swap(total, "row", k).reshape(2 * zs, n, I) for k in range(R)]

    def grad_rows():
        stacked = jnp.stack(out_r, axis=0).reshape(R, Z, 2, n, K_out)

        def half(rcore):
            h = stacked[:, :, rcore]
            t = h[:, :, :nt].transpose(1, 0, 2, 3).reshape(Z, R * nt, K_out)
            q = h[:, :, nt:].transpose(1, 0, 2, 3).reshape(Z, R * nq, K_out)
            return jnp.concatenate([t, q], axis=1).reshape(Z * R * n, K_out)

        return half(0), half(1)

    starts = [sum(CHUNKS[:c]) * O // sum(CHUNKS) for c in range(len(CHUNKS) + 1)]

    def send_grads(c, mine, other):
        basis = output_basis[:, starts[c]:starts[c + 1]]
        sent = jnp.dot(other, basis, preferred_element_type=f32)
        got = swap(sent, "col", 1)
        kept = jnp.dot(mine, basis, preferred_element_type=f32)
        both = (kept + got).reshape(Z, R * n, -1)
        parts = [both[0]] + [both[z].astype(bf16) for z in range(1, Z)]
        return [swap(p, "col", 2 * z) for z, p in enumerate(parts)]

    def share_grads(got):
        got = [got[0]] + [p.astype(f32) for p in got[1:]]
        total = tree_sum(got).astype(bf16)
        own = [swap(total, "col", 2 * z) for z in range(Z)]
        theirs = [swap(p, "col", 1) for p in own]
        return [p for two in zip(own, theirs) for p in two]

    in_got = [send_inputs(g) for g in range(GROUPS)]
    mine, other = grad_rows()
    sums = [send_grads(c, mine, other) for c in range(len(CHUNKS))]
    shared = [share_inputs(got) for got in in_got]
    grad_pieces = [share_grads(got) for got in sums]
    ti = jnp.concatenate([jnp.stack([p[:, :nt] for p in rot], axis=1) for rot in shared], axis=0)
    qi = jnp.concatenate([jnp.stack([p[:, nt:] for p in rot], axis=1) for rot in shared], axis=0)
    ti, qi = ti.reshape(R * C * nt, I), qi.reshape(R * C * nq, I)

    scores = None
    for c in range(len(CHUNKS)):
        scores = score(spans, ti, qi, scores, eigenvalues, grad_pieces[c], starts[c],
                       n_queries, (R, C, nt, nq), c == len(CHUNKS) - 1)

    scores = scores + swap(scores, "col", 1)
    scores = tree_sum([swap(scores, "col", 2 * z) for z in range(Z)])
    scores = tree_sum([swap(scores, "row", k) for k in range(R)])
    return scores * (1.0 / math.sqrt(K_in * R * O * R * QBLOCK))


def solution(mesh):
    in_specs = (
        P(("row", "col"), None),
        P(("row", "col"), None),
        P(("row", "col"), None),
        P(("row", "col"), None),
        P("row", "col"),
        P("col", "row"),
        P("row", "col"),
        P(),
        P(),
    )

    return jax.shard_map(shards, mesh=mesh, in_specs=in_specs, out_specs=P(), check_vma=False)
```

time: 643 us -> 298 us (0.46)
  blocking collectives: 310 us -> 0 us
  matrix products: 161 us -> 10.7 us
  waiting for transfers between devices: 37.4 us -> 135 us
  starting transfers between devices: 10.7 us -> 75 us
  Pallas kernels: 0 us -> 62.3 us
  loops' own time: 41.6 us -> 0 us
  other arithmetic: 30.5 us -> 3.97 us
  local copies, waits for them, and re-layouts: 36.4 us -> 9.97 us
  between operations: 13.2 us -> 0.74 us
    psum x3 -> x0, blocking collectives: 279 us -> none  [the longest x1 129 us: shards(): out_sums = lax.psum((train_out_part, query_out_part), 'col')]
    dot_general x20 -> x12, matrix products: 161 us -> 10.7 us  [the longest x8 6.52 us: send_inputs(): parts.append(jnp.dot(rows[k], input_basis, preferred_element_type=f32))]
    ppermute x0 -> x58, waiting for transfers between devices: none -> 135 us  [swap(): lax.ppermute(x, axis, [(i, i ^ k) for i in range(lax.axis_size(axis))])]
    ppermute x0 -> x58, starting transfers between devices: none -> 75 us  [swap(): lax.ppermute(x, axis, [(i, i ^ k) for i in range(lax.axis_size(axis))])]
    pallas_call x0 -> x2, Pallas kernels: none -> 62.3 us  [score(): pl.pallas_call(functools.partial(score_kernel, n_queries=n_queries, sizes...]
    another operation x1 -> x0, loops' own time: 41.6 us -> none  [shards(): partial_scores = lax.map(per_query, (query_starts, query_ends))]
    all_gather x3 -> x0, waiting for transfers between devices: 36 us -> none  [the longest x1 24 us: shards(): lax.all_gather(train_inputs, 'col', axis=0, tiled=True)]
    and x16 -> x0, other arithmetic: 21.2 us -> none  [per_query(): inside = (positions >= span_start) & (positions < span_end)]
  transfers between devices with their start and end apart: 6 -> 58, of which waited for: 2 -> 28; matrix products, arithmetic and copies ran while one was open for 6% -> 5% of each run, Pallas kernels for 0% -> 10%
where the time goes in v1:
time: 298 us; the launch traced here: 297 us
  waiting for transfers between devices  135 us (45%)
  starting transfers between devices  75 us (25%)
  Pallas kernels  62.3 us (21%)
  matrix products  10.7 us (4%)
  local copies, waits for them, and re-layouts  9.97 us (3%)
  other arithmetic  3.97 us (1%)
    ppermute x58, waiting for transfers between devices, swap(): lax.ppermute(x, axis, [(i, i ^ k) for i in range(lax.axis_size(axis))])  135 us
    ppermute x58, starting transfers between devices, swap(): lax.ppermute(x, axis, [(i, i ^ k) for i in range(lax.axis_size(axis))])  75 us
    pallas_call x2, Pallas kernels, score(): pl.pallas_call(functools.partial(score_kernel, n_queries=n_queries, sizes...  62.3 us
    unnamed x48, local copies, waits for them, and re-layouts  7.02 us
    dot_general x8, matrix products, send_inputs(): parts.append(jnp.dot(rows[k], input_basis, preferred_element_type=f32))  6.52 us
  transfers between devices with their start and end apart: 58, of which 28 were waited for; matrix products, arithmetic and copies ran while one was open for 5% of the time, Pallas kernels for 10%

profile of v1, /device:TPU:0, one launch (start us, length us, event | category | flops | bytes accessed | tf_op | source)
XLA Modules:
  0.0 297.4 jit_solution(17941447572316097940)
XLA Ops:
  2.0 4.0 %collective-permute-start.2 = (bf16[24,2048]{1,0:T(8,128)(2,1)S(1)}, bf16[24,2048]{1,0:T(8,128)(2,1)S(1)}, u32[]{:S(2)}, u32[]{:S(2)}) collective-permute-start(bf16[24,2048]{1,0:T(8,128)(2,1)S(1)} %get-tuple-element.30), channel_id=1, source_target_pairs={{0,24},{8,16},{16,8},{24,0},{1,25},{9,17},{17,9},{25,1},{2,26},{10... | collective-permute-start | bytes 294920 | tf_op jit(solution)/shard_map/ppermute | solution.py:22
  6.9 2.3 collective-permute-done.2
  11.3 3.7 %collective-permute-start.14 = (bf16[96,2048]{1,0:T(8,128)(2,1)S(1)}, bf16[96,2048]{1,0:T(8,128)(2,1)S(1)}, u32[]{:S(2)}, u32[]{:S(2)}) collective-permute-start(bf16[96,2048]{1,0:T(8,128)(2,1)S(1)} %pad_maximum_fusion.5), channel_id=1, source_target_pairs={{0,6},{1,7},{2,4},{3,5},{4,2},{5,3},{6,0},{7,1},{8,14},{9,15},{10,... | collective-permute-start | bytes 1179656 | tf_op jit(solution)/shard_map/ppermute | solution.py:22
  17.1 3.0 %collective-permute-start.24 = (bf16[48,1024]{1,0:T(8,128)(2,1)S(1)}, bf16[48,1024]{1,0:T(8,128)(2,1)S(1)}, u32[]{:S(2)}, u32[]{:S(2)}) collective-permute-start(bf16[48,1024]{1,0:T(8,128)(2,1)S(1)} %pad_maximum_fusion.9), channel_id=1, source_target_pairs={{0,4},{1,5},{2,6},{3,7},{4,0},{5,1},{6,2},{7,3},{8,12},{9,13},{10,... | collective-permute-start | bytes 294920 | tf_op jit(solution)/shard_map/ppermute | solution.py:22
  20.1 23.4 %collective-permute-done.23 = bf16[48,1024]{1,0:T(8,128)(2,1)S(1)} collective-permute-done((bf16[48,1024]{1,0:T(8,128)(2,1)S(1)}, bf16[48,1024]{1,0:T(8,128)(2,1)S(1)}, u32[]{:S(2)}, u32[]{:S(2)}) %collective-permute-start.23) | collective-permute-done | bytes 98336 | tf_op jit(solution)/shard_map/ppermute | solution.py:22
  43.5 12.0 %collective-permute-done.24 = bf16[48,1024]{1,0:T(8,128)(2,1)S(1)} collective-permute-done((bf16[48,1024]{1,0:T(8,128)(2,1)S(1)}, bf16[48,1024]{1,0:T(8,128)(2,1)S(1)}, u32[]{:S(2)}, u32[]{:S(2)}) %collective-permute-start.24) | collective-permute-done | bytes 98336 | tf_op jit(solution)/shard_map/ppermute | solution.py:22
  56.5 2.2 collective-permute-start.27
  60.2 8.3 %collective-permute-done.28 = bf16[192,1024]{1,0:T(8,128)(2,1)S(1)} collective-permute-done((bf16[192,1024]{1,0:T(8,128)(2,1)S(1)}, bf16[192,1024]{1,0:T(8,128)(2,1)S(1)}, u32[]{:S(2)}, u32[]{:S(2)}) %collective-permute-start.28) | collective-permute-done | bytes 393248 | tf_op jit(solution)/shard_map/ppermute | solution.py:22
  68.5 5.7 %collective-permute-done.27 = bf16[192,1024]{1,0:T(8,128)(2,1)S(1)} collective-permute-done((bf16[192,1024]{1,0:T(8,128)(2,1)S(1)}, bf16[192,1024]{1,0:T(8,128)(2,1)S(1)}, u32[]{:S(2)}, u32[]{:S(2)}) %collective-permute-start.27) | collective-permute-done | bytes 393248 | tf_op jit(solution)/shard_map/ppermute | solution.py:22
  90.8 4.0 %collective-permute-done.16 = f32[96,1024]{1,0:T(8,128)S(1)} collective-permute-done((f32[96,1024]{1,0:T(8,128)S(1)}, f32[96,1024]{1,0:T(8,128)S(1)}, u32[]{:S(2)}, u32[]{:S(2)}) %collective-permute-start.16) | collective-permute-done | bytes 393248 | tf_op jit(solution)/shard_map/ppermute | solution.py:22
  96.3 9.4 %collective-permute-done.17 = f32[96,1024]{1,0:T(8,128)S(1)} collective-permute-done((f32[96,1024]{1,0:T(8,128)S(1)}, f32[96,1024]{1,0:T(8,128)S(1)}, u32[]{:S(2)}, u32[]{:S(2)}) %collective-permute-start.17) | collective-permute-done | bytes 393248 | tf_op jit(solution)/shard_map/ppermute | solution.py:22
  108.3 3.5 %collective-permute-done.6 = f32[96,1024]{1,0:T(8,128)S(1)} collective-permute-done((f32[96,1024]{1,0:T(8,128)S(1)}, f32[96,1024]{1,0:T(8,128)S(1)}, u32[]{:S(2)}, u32[]{:S(2)}) %collective-permute-start.6) | collective-permute-done | bytes 393248 | tf_op jit(solution)/shard_map/ppermute | solution.py:22
  113.2 15.5 %collective-permute-done.7 = f32[96,1024]{1,0:T(8,128)S(1)} collective-permute-done((f32[96,1024]{1,0:T(8,128)S(1)}, f32[96,1024]{1,0:T(8,128)S(1)}, u32[]{:S(2)}, u32[]{:S(2)}) %collective-permute-start.7) | collective-permute-done | bytes 393248 | tf_op jit(solution)/shard_map/ppermute | solution.py:22
  133.1 4.3 %collective-permute-done.20 = bf16[96,1024]{1,0:T(8,128)(2,1)S(1)} collective-permute-done((bf16[96,1024]{1,0:T(8,128)(2,1)S(1)}, bf16[96,1024]{1,0:T(8,128)(2,1)S(1)}, u32[]{:S(2)}, u32[]{:S(2)}) %collective-permute-start.20) | collective-permute-done | bytes 196640 | tf_op jit(solution)/shard_map/ppermute | solution.py:22
  141.6 2.0 collective-permute-done.10
  144.7 2.3 collective-permute-start.32
  150.4 2.3 collective-permute-start.43
  154.5 12.6 %collective-permute-start.41 = (bf16[96,1024]{1,0:T(8,128)(2,1)S(1)}, bf16[96,1024]{1,0:T(8,128)(2,1)S(1)}, u32[]{:S(2)}, u32[]{:S(2)}) collective-permute-start(bf16[96,1024]{1,0:T(8,128)(2,1)S(1)} %get-tuple-element.15), channel_id=1, source_target_pairs={{0,2},{1,3},{2,0},{3,1},{4,6},{5,7},{6,4},{7,5},{8,10},{9,11},{10,... | collective-permute-start | bytes 589832 | tf_op jit(solution)/shard_map/ppermute | solution.py:22
  167.1 4.3 %collective-permute-done.31 = bf16[96,1024]{1,0:T(8,128)(2,1)S(1)} collective-permute-done((bf16[96,1024]{1,0:T(8,128)(2,1)S(1)}, bf16[96,1024]{1,0:T(8,128)(2,1)S(1)}, u32[]{:S(2)}, u32[]{:S(2)}) %collective-permute-start.31) | collective-permute-done | bytes 196640 | tf_op jit(solution)/shard_map/ppermute | solution.py:22
  171.7 5.1 %collective-permute-start.36 = (bf16[96,1024]{1,0:T(8,128)(2,1)S(1)}, bf16[96,1024]{1,0:T(8,128)(2,1)S(1)}, u32[]{:S(2)}, u32[]{:S(2)}) collective-permute-start(bf16[96,1024]{1,0:T(8,128)(2,1)S(1)} %fusion.21.refs_1_), channel_id=1, source_target_pairs={{0,4},{1,5},{2,6},{3,7},{4,0},{5,1},{6,2},{7,3},{8,12},{9,13},{10,... | collective-permute-start | bytes 589832 | tf_op jit(solution)/shard_map/ppermute | solution.py:22
  176.8 7.3 %collective-permute-done.42 = bf16[96,1024]{1,0:T(8,128)(2,1)S(1)} collective-permute-done((bf16[96,1024]{1,0:T(8,128)(2,1)S(1)}, bf16[96,1024]{1,0:T(8,128)(2,1)S(1)}, u32[]{:S(2)}, u32[]{:S(2)}) %collective-permute-start.42) | collective-permute-done | bytes 196640 | tf_op jit(solution)/shard_map/ppermute | solution.py:22
  184.1 2.1 collective-permute-start.38
  186.4 2.3 collective-permute-start.47
  188.6 2.1 collective-permute-start.49
  191.3 2.4 collective-permute-done.38.refs_7_
  193.7 2.3 collective-permute-done.45.refs_4_
  196.0 13.3 %collective-permute-done.47.refs_6_ = bf16[96,1024]{1,0:T(8,128)(2,1)S(1)} collective-permute-done((bf16[96,1024]{1,0:T(8,128)(2,1)S(1)}, bf16[96,1024]{1,0:T(8,128)(2,1)S(1)}, u32[]{:S(2)}, u32[]{:S(2)}) %collective-permute-start.47) | collective-permute-done | bytes 196640 | tf_op jit(solution)/shard_map/ppermute | solution.py:22
  213.2 30.6 %shard_map.91.refs_0_ = f32[16,512]{1,0:T(8,128)} custom-call(s32[34]{0:T(128)} %pad_add_fusion.spans, bf16[512,1024]{1,0:T(8,128)(2,1)} %bitcast.112, bf16[256,1024]{1,0:T(8,128)(2,1)} %bitcast.116, f32[2048,1024]{1,0:T(8,128)} %refs_1_.1, bf16[96,1024]{1,0:T(8,128)(2,1)} %copy-done.2, bf16[96,1024]{1,0:T(8,128)(2,1)} %copy-done.5, ...), custom_call_target="tpu_custom_call" | custom-call | tf_op jit(solution)/shard_map/pallas_call | solution.py:83
  245.4 31.7 %shard_map.92 = f32[16,512]{1,0:T(8,128)} custom-call(s32[34]{0:T(128)} %pad_add_fusion.spans, bf16[512,1024]{1,0:T(8,128)(2,1)} %bitcast.113, bf16[256,1024]{1,0:T(8,128)(2,1)} %bitcast.117, f32[16,512]{1,0:T(8,128)} %shard_map.91.refs_0_, f32[2048,1024]{1,0:T(8,128)} %refs_1_.1, bf16[96,1024]{1,0:T(8,128)(2,1)} %copy-done.3, bf16[96,1024]{1,0:T(8,128)(2,1)} %copy-done.12, ...), custom_call_target="tpu_custom_call" | custom-call | tf_op jit(solution)/shard_map/pallas_call | solution.py:83
  279.2 4.7 %collective-permute-start.53 = (f32[16,512]{1,0:T(8,128)S(1)}, f32[16,512]{1,0:T(8,128)S(1)}, u32[]{:S(2)}, u32[]{:S(2)}) collective-permute-start(f32[16,512]{1,0:T(8,128)S(1)} %add.125), channel_id=1, source_target_pairs={{0,4},{1,5},{2,6},{3,7},{4,0},{5,1},{6,2},{7,3},{8,12},{9,13},{10,... | collective-permute-start | bytes 98312 | tf_op jit(solution)/shard_map/ppermute | solution.py:22
  286.2 3.5 %collective-permute-done.54 = f32[16,512]{1,0:T(8,128)S(1)} collective-permute-done((f32[16,512]{1,0:T(8,128)S(1)}, f32[16,512]{1,0:T(8,128)S(1)}, u32[]{:S(2)}, u32[]{:S(2)}) %collective-permute-start.54) | collective-permute-done | bytes 32800 | tf_op jit(solution)/shard_map/ppermute | solution.py:22
  293.6 2.6 collective-permute-done.57
  (197 shorter events, 62.2 us)
Async XLA Ops:
  11.3 47.5 %collective-permute-start.14 = (bf16[96,2048]{1,0:T(8,128)(2,1)S(1)}, bf16[96,2048]{1,0:T(8,128)(2,1)S(1)}, u32[]{:S(2)}, u32[]{:S(2)}) collective-permute-start(bf16[96,2048]{1,0:T(8,128)(2,1)S(1)} %pad_maximum_fusion.5), channel_id=1, source_target_pairs={{0,6},{1,7},{2,4},{3,5},{4,2},{5,3},{6,0},{7,1},{8,14},{9,15},{10,... | collective-permute-start | bytes 1179656 | tf_op jit(solution)/shard_map/ppermute | solution.py:22
  14.9 44.8 %collective-permute-start.12 = (bf16[96,2048]{1,0:T(8,128)(2,1)S(1)}, bf16[96,2048]{1,0:T(8,128)(2,1)S(1)}, u32[]{:S(2)}, u32[]{:S(2)}) collective-permute-start(bf16[96,2048]{1,0:T(8,128)(2,1)S(1)} %pad_maximum_fusion.5), channel_id=1, source_target_pairs={{0,4},{1,5},{2,6},{3,7},{4,0},{5,1},{6,2},{7,3},{8,12},{9,13},{10,... | collective-permute-start | bytes 1179656 | tf_op jit(solution)/shard_map/ppermute | solution.py:22
  14.9 44.8 %collective-permute-start.4 = (bf16[96,2048]{1,0:T(8,128)(2,1)S(1)}, bf16[96,2048]{1,0:T(8,128)(2,1)S(1)}, u32[]{:S(2)}, u32[]{:S(2)}) collective-permute-start(bf16[96,2048]{1,0:T(8,128)(2,1)S(1)} %pad_maximum_fusion.5), channel_id=1, source_target_pairs={{0,2},{1,3},{2,0},{3,1},{4,6},{5,7},{6,4},{7,5},{8,10},{9,11},{10,... | collective-permute-start | bytes 1179656 | tf_op jit(solution)/shard_map/ppermute | solution.py:22
  15.8 27.7 %collective-permute-start.23 = (bf16[48,1024]{1,0:T(8,128)(2,1)S(1)}, bf16[48,1024]{1,0:T(8,128)(2,1)S(1)}, u32[]{:S(2)}, u32[]{:S(2)}) collective-permute-start(bf16[48,1024]{1,0:T(8,128)(2,1)S(1)} %pad_maximum_fusion.8), channel_id=1, source_target_pairs={{0,2},{1,3},{2,0},{3,1},{4,6},{5,7},{6,4},{7,5},{8,10},{9,11},{10,... | collective-permute-start | bytes 294920 | tf_op jit(solution)/shard_map/ppermute | solution.py:22
  17.1 38.4 %collective-permute-start.24 = (bf16[48,1024]{1,0:T(8,128)(2,1)S(1)}, bf16[48,1024]{1,0:T(8,128)(2,1)S(1)}, u32[]{:S(2)}, u32[]{:S(2)}) collective-permute-start(bf16[48,1024]{1,0:T(8,128)(2,1)S(1)} %pad_maximum_fusion.9), channel_id=1, source_target_pairs={{0,4},{1,5},{2,6},{3,7},{4,0},{5,1},{6,2},{7,3},{8,12},{9,13},{10,... | collective-permute-start | bytes 294920 | tf_op jit(solution)/shard_map/ppermute | solution.py:22
  56.5 17.6 %collective-permute-start.27 = (bf16[192,1024]{1,0:T(8,128)(2,1)S(1)}, bf16[192,1024]{1,0:T(8,128)(2,1)S(1)}, u32[]{:S(2)}, u32[]{:S(2)}) collective-permute-start(bf16[192,1024]{1,0:T(8,128)(2,1)S(1)} %constant_dynamic-update-slice_fusion.4), channel_id=1, source_target_pairs={{0,16},{8,24},{16,0},{24,8},{1,17},{9,25},{17,1},{25,9},{2,18},{10... | collective-permute-start | bytes 1179656 | tf_op jit(solution)/shard_map/ppermute | solution.py:22
  58.7 15.7 %collective-permute-start.26 = (bf16[192,1024]{1,0:T(8,128)(2,1)S(1)}, bf16[192,1024]{1,0:T(8,128)(2,1)S(1)}, u32[]{:S(2)}, u32[]{:S(2)}) collective-permute-start(bf16[192,1024]{1,0:T(8,128)(2,1)S(1)} %constant_dynamic-update-slice_fusion.4), channel_id=1, source_target_pairs={{0,8},{8,0},{16,24},{24,16},{1,9},{9,1},{17,25},{25,17},{2,10},{10... | collective-permute-start | bytes 1179656 | tf_op jit(solution)/shard_map/ppermute | solution.py:22
  59.7 26.2 %collective-permute-start.3 = (bf16[96,2048]{1,0:T(8,128)(2,1)S(1)}, bf16[96,2048]{1,0:T(8,128)(2,1)S(1)}, u32[]{:S(2)}, u32[]{:S(2)}) collective-permute-start(bf16[96,2048]{1,0:T(8,128)(2,1)S(1)} %pad_maximum_fusion.5), channel_id=1, source_target_pairs={{0,1},{1,0},{2,3},{3,2},{4,5},{5,4},{6,7},{7,6},{8,9},{9,8},{10,11... | collective-permute-start | bytes 1179656 | tf_op jit(solution)/shard_map/ppermute | solution.py:22
  59.7 19.7 %collective-permute-start.15 = (bf16[96,2048]{1,0:T(8,128)(2,1)S(1)}, bf16[96,2048]{1,0:T(8,128)(2,1)S(1)}, u32[]{:S(2)}, u32[]{:S(2)}) collective-permute-start(bf16[96,2048]{1,0:T(8,128)(2,1)S(1)} %collective-permute-done.14), channel_id=1, source_target_pairs={{0,1},{1,0},{2,3},{3,2},{4,5},{5,4},{6,7},{7,6},{8,9},{9,8},{10,11... | collective-permute-start | bytes 1179656 | tf_op jit(solution)/shard_map/ppermute | solution.py:22
  78.0 65.6 %collective-permute-start.29 = (f32[384,1024]{1,0:T(8,128)S(1)}, f32[384,1024]{1,0:T(8,128)S(1)}, u32[]{:S(2)}, u32[]{:S(2)}) collective-permute-start(f32[384,1024]{1,0:T(8,128)S(1)} %fusion.4), channel_id=1, source_target_pairs={{0,1},{1,0},{2,3},{3,2},{4,5},{5,4},{6,7},{7,6},{8,9},{9,8},{10,11... | collective-permute-start | bytes 4718600 | tf_op jit(solution)/shard_map/ppermute | solution.py:22
  79.4 69.8 %collective-permute-start.40 = (f32[384,1024]{1,0:T(8,128)S(1)}, f32[384,1024]{1,0:T(8,128)S(1)}, u32[]{:S(2)}, u32[]{:S(2)}) collective-permute-start(f32[384,1024]{1,0:T(8,128)S(1)} %fusion), channel_id=1, source_target_pairs={{0,1},{1,0},{2,3},{3,2},{4,5},{5,4},{6,7},{7,6},{8,9},{9,8},{10,11... | collective-permute-start | bytes 4718600 | tf_op jit(solution)/shard_map/ppermute | solution.py:22
  85.9 19.7 %collective-permute-start.17 = (f32[96,1024]{1,0:T(8,128)S(1)}, f32[96,1024]{1,0:T(8,128)S(1)}, u32[]{:S(2)}, u32[]{:S(2)}) collective-permute-start(f32[96,1024]{1,0:T(8,128)S(1)} %fusion.33), channel_id=1, source_target_pairs={{0,16},{8,24},{16,0},{24,8},{1,17},{9,25},{17,1},{25,9},{2,18},{10... | collective-permute-start | bytes 1179656 | tf_op jit(solution)/shard_map/ppermute | solution.py:22
  86.5 19.4 %collective-permute-start.18 = (f32[96,1024]{1,0:T(8,128)S(1)}, f32[96,1024]{1,0:T(8,128)S(1)}, u32[]{:S(2)}, u32[]{:S(2)}) collective-permute-start(f32[96,1024]{1,0:T(8,128)S(1)} %fusion.34), channel_id=1, source_target_pairs={{0,24},{8,16},{16,8},{24,0},{1,25},{9,17},{17,9},{25,1},{2,26},{10... | collective-permute-start | bytes 1179656 | tf_op jit(solution)/shard_map/ppermute | solution.py:22
  94.8 16.9 %collective-permute-start.6 = (f32[96,1024]{1,0:T(8,128)S(1)}, f32[96,1024]{1,0:T(8,128)S(1)}, u32[]{:S(2)}, u32[]{:S(2)}) collective-permute-start(f32[96,1024]{1,0:T(8,128)S(1)} %fusion.29), channel_id=1, source_target_pairs={{0,8},{8,0},{16,24},{24,16},{1,9},{9,1},{17,25},{25,17},{2,10},{10... | collective-permute-start | bytes 1179656 | tf_op jit(solution)/shard_map/ppermute | solution.py:22
  105.6 23.0 %collective-permute-start.7 = (f32[96,1024]{1,0:T(8,128)S(1)}, f32[96,1024]{1,0:T(8,128)S(1)}, u32[]{:S(2)}, u32[]{:S(2)}) collective-permute-start(f32[96,1024]{1,0:T(8,128)S(1)} %fusion.30), channel_id=1, source_target_pairs={{0,16},{8,24},{16,0},{24,8},{1,17},{9,25},{17,1},{25,9},{2,18},{10... | collective-permute-start | bytes 1179656 | tf_op jit(solution)/shard_map/ppermute | solution.py:22
  105.9 23.0 %collective-permute-start.8 = (f32[96,1024]{1,0:T(8,128)S(1)}, f32[96,1024]{1,0:T(8,128)S(1)}, u32[]{:S(2)}, u32[]{:S(2)}) collective-permute-start(f32[96,1024]{1,0:T(8,128)S(1)} %fusion.31), channel_id=1, source_target_pairs={{0,24},{8,16},{16,8},{24,0},{1,25},{9,17},{17,9},{25,1},{2,26},{10... | collective-permute-start | bytes 1179656 | tf_op jit(solution)/shard_map/ppermute | solution.py:22
  111.7 19.8 %collective-permute-start.21 = (bf16[96,1024]{1,0:T(8,128)(2,1)S(1)}, bf16[96,1024]{1,0:T(8,128)(2,1)S(1)}, u32[]{:S(2)}, u32[]{:S(2)}) collective-permute-start(bf16[96,1024]{1,0:T(8,128)(2,1)S(1)} %fusion.16), channel_id=1, source_target_pairs={{0,24},{8,16},{16,8},{24,0},{1,25},{9,17},{17,9},{25,1},{2,26},{10... | collective-permute-start | bytes 589832 | tf_op jit(solution)/shard_map/ppermute | solution.py:22
  147.0 24.4 %collective-permute-start.31 = (bf16[96,1024]{1,0:T(8,128)(2,1)S(1)}, bf16[96,1024]{1,0:T(8,128)(2,1)S(1)}, u32[]{:S(2)}, u32[]{:S(2)}) collective-permute-start(bf16[96,1024]{1,0:T(8,128)(2,1)S(1)} %get-tuple-element.20), channel_id=1, source_target_pairs={{0,4},{1,5},{2,6},{3,7},{4,0},{5,1},{6,2},{7,3},{8,12},{9,13},{10,... | collective-permute-start | bytes 589832 | tf_op jit(solution)/shard_map/ppermute | solution.py:22
  148.9 22.5 %collective-permute-start.30 = (bf16[96,1024]{1,0:T(8,128)(2,1)S(1)}, bf16[96,1024]{1,0:T(8,128)(2,1)S(1)}, u32[]{:S(2)}, u32[]{:S(2)}) collective-permute-start(bf16[96,1024]{1,0:T(8,128)(2,1)S(1)} %get-tuple-element.18), channel_id=1, source_target_pairs={{0,2},{1,3},{2,0},{3,1},{4,6},{5,7},{6,4},{7,5},{8,10},{9,11},{10,... | collective-permute-start | bytes 589832 | tf_op jit(solution)/shard_map/ppermute | solution.py:22
  150.4 21.2 %collective-permute-start.43 = (bf16[96,1024]{1,0:T(8,128)(2,1)S(1)}, bf16[96,1024]{1,0:T(8,128)(2,1)S(1)}, u32[]{:S(2)}, u32[]{:S(2)}) collective-permute-start(bf16[96,1024]{1,0:T(8,128)(2,1)S(1)} %get-tuple-element.16), channel_id=1, source_target_pairs={{0,6},{1,7},{2,4},{3,5},{4,2},{5,3},{6,0},{7,1},{8,14},{9,15},{10,... | collective-permute-start | bytes 589832 | tf_op jit(solution)/shard_map/ppermute | solution.py:22
  152.7 31.3 %collective-permute-start.42 = (bf16[96,1024]{1,0:T(8,128)(2,1)S(1)}, bf16[96,1024]{1,0:T(8,128)(2,1)S(1)}, u32[]{:S(2)}, u32[]{:S(2)}) collective-permute-start(bf16[96,1024]{1,0:T(8,128)(2,1)S(1)} %get-tuple-element.17), channel_id=1, source_target_pairs={{0,4},{1,5},{2,6},{3,7},{4,0},{5,1},{6,2},{7,3},{8,12},{9,13},{10,... | collective-permute-start | bytes 589832 | tf_op jit(solution)/shard_map/ppermute | solution.py:22
  154.5 31.7 %collective-permute-start.41 = (bf16[96,1024]{1,0:T(8,128)(2,1)S(1)}, bf16[96,1024]{1,0:T(8,128)(2,1)S(1)}, u32[]{:S(2)}, u32[]{:S(2)}) collective-permute-start(bf16[96,1024]{1,0:T(8,128)(2,1)S(1)} %get-tuple-element.15), channel_id=1, source_target_pairs={{0,2},{1,3},{2,0},{3,1},{4,6},{5,7},{6,4},{7,5},{8,10},{9,11},{10,... | collective-permute-start | bytes 589832 | tf_op jit(solution)/shard_map/ppermute | solution.py:22
  171.6 17.1 %collective-permute-start.34 = (bf16[96,1024]{1,0:T(8,128)(2,1)S(1)}, bf16[96,1024]{1,0:T(8,128)(2,1)S(1)}, u32[]{:S(2)}, u32[]{:S(2)}) collective-permute-start(bf16[96,1024]{1,0:T(8,128)(2,1)S(1)} %fusion.21.refs_1_), channel_id=1, source_target_pairs={{0,2},{1,3},{2,0},{3,1},{4,6},{5,7},{6,4},{7,5},{8,10},{9,11},{10,... | collective-permute-start | bytes 589832 | tf_op jit(solution)/shard_map/ppermute | solution.py:22
  171.7 19.7 %collective-permute-start.36 = (bf16[96,1024]{1,0:T(8,128)(2,1)S(1)}, bf16[96,1024]{1,0:T(8,128)(2,1)S(1)}, u32[]{:S(2)}, u32[]{:S(2)}) collective-permute-start(bf16[96,1024]{1,0:T(8,128)(2,1)S(1)} %fusion.21.refs_1_), channel_id=1, source_target_pairs={{0,4},{1,5},{2,6},{3,7},{4,0},{5,1},{6,2},{7,3},{8,12},{9,13},{10,... | collective-permute-start | bytes 589832 | tf_op jit(solution)/shard_map/ppermute | solution.py:22
  186.4 23.0 %collective-permute-start.47 = (bf16[96,1024]{1,0:T(8,128)(2,1)S(1)}, bf16[96,1024]{1,0:T(8,128)(2,1)S(1)}, u32[]{:S(2)}, u32[]{:S(2)}) collective-permute-start(bf16[96,1024]{1,0:T(8,128)(2,1)S(1)} %fusion.19.refs_2_), channel_id=1, source_target_pairs={{0,4},{1,5},{2,6},{3,7},{4,0},{5,1},{6,2},{7,3},{8,12},{9,13},{10,... | collective-permute-start | bytes 589832 | tf_op jit(solution)/shard_map/ppermute | solution.py:22
  188.6 20.7 %collective-permute-start.49 = (bf16[96,1024]{1,0:T(8,128)(2,1)S(1)}, bf16[96,1024]{1,0:T(8,128)(2,1)S(1)}, u32[]{:S(2)}, u32[]{:S(2)}) collective-permute-start(bf16[96,1024]{1,0:T(8,128)(2,1)S(1)} %fusion.19.refs_2_), channel_id=1, source_target_pairs={{0,6},{1,7},{2,4},{3,5},{4,2},{5,3},{6,0},{7,1},{8,14},{9,15},{10,... | collective-permute-start | bytes 589832 | tf_op jit(solution)/shard_map/ppermute | solution.py:22
  191.3 18.5 %collective-permute-start.35 = (bf16[96,1024]{1,0:T(8,128)(2,1)S(1)}, bf16[96,1024]{1,0:T(8,128)(2,1)S(1)}, u32[]{:S(2)}, u32[]{:S(2)}) collective-permute-start(bf16[96,1024]{1,0:T(8,128)(2,1)S(1)} %collective-permute-done.34.refs_3_), channel_id=1, source_target_pairs={{0,1},{1,0},{2,3},{3,2},{4,5},{5,4},{6,7},{7,6},{8,9},{9,8},{10,11... | collective-permute-start | bytes 589832 | tf_op jit(solution)/shard_map/ppermute | solution.py:22
  193.7 16.2 %collective-permute-start.37 = (bf16[96,1024]{1,0:T(8,128)(2,1)S(1)}, bf16[96,1024]{1,0:T(8,128)(2,1)S(1)}, u32[]{:S(2)}, u32[]{:S(2)}) collective-permute-start(bf16[96,1024]{1,0:T(8,128)(2,1)S(1)} %collective-permute-done.36.refs_5_), channel_id=1, source_target_pairs={{0,1},{1,0},{2,3},{3,2},{4,5},{5,4},{6,7},{7,6},{8,9},{9,8},{10,11... | collective-permute-start | bytes 589832 | tf_op jit(solution)/shard_map/ppermute | solution.py:22
  196.0 47.9 %collective-permute-start.44 = (bf16[96,1024]{1,0:T(8,128)(2,1)S(1)}, bf16[96,1024]{1,0:T(8,128)(2,1)S(1)}, u32[]{:S(2)}, u32[]{:S(2)}) collective-permute-start(bf16[96,1024]{1,0:T(8,128)(2,1)S(1)} %fusion.19.refs_2_), channel_id=1, source_target_pairs={{0,1},{1,0},{2,3},{3,2},{4,5},{5,4},{6,7},{7,6},{8,9},{9,8},{10,11... | collective-permute-start | bytes 589832 | tf_op jit(solution)/shard_map/ppermute | solution.py:22
  209.4 34.5 %collective-permute-start.46 = (bf16[96,1024]{1,0:T(8,128)(2,1)S(1)}, bf16[96,1024]{1,0:T(8,128)(2,1)S(1)}, u32[]{:S(2)}, u32[]{:S(2)}) collective-permute-start(bf16[96,1024]{1,0:T(8,128)(2,1)S(1)} %collective-permute-done.45.refs_4_), channel_id=1, source_target_pairs={{0,1},{1,0},{2,3},{3,2},{4,5},{5,4},{6,7},{7,6},{8,9},{9,8},{10,11... | collective-permute-start | bytes 589832 | tf_op jit(solution)/shard_map/ppermute | solution.py:22
  209.9 34.0 %collective-permute-start.48 = (bf16[96,1024]{1,0:T(8,128)(2,1)S(1)}, bf16[96,1024]{1,0:T(8,128)(2,1)S(1)}, u32[]{:S(2)}, u32[]{:S(2)}) collective-permute-start(bf16[96,1024]{1,0:T(8,128)(2,1)S(1)} %collective-permute-done.47.refs_6_), channel_id=1, source_target_pairs={{0,1},{1,0},{2,3},{3,2},{4,5},{5,4},{6,7},{7,6},{8,9},{9,8},{10,11... | collective-permute-start | bytes 589832 | tf_op jit(solution)/shard_map/ppermute | solution.py:22
  210.0 34.0 %collective-permute-start.50 = (bf16[96,1024]{1,0:T(8,128)(2,1)S(1)}, bf16[96,1024]{1,0:T(8,128)(2,1)S(1)}, u32[]{:S(2)}, u32[]{:S(2)}) collective-permute-start(bf16[96,1024]{1,0:T(8,128)(2,1)S(1)} %collective-permute-done.49.refs_8_), channel_id=1, source_target_pairs={{0,1},{1,0},{2,3},{3,2},{4,5},{5,4},{6,7},{7,6},{8,9},{9,8},{10,11... | collective-permute-start | bytes 589832 | tf_op jit(solution)/shard_map/ppermute | solution.py:22
  (48 other events, 504.8 us)
